TPU v7x, 256 devices: a whole 4x4x8 slice. The times are simulated.
256 devices in a mesh: island: 4 (over z_hi, core), tensor: 64 (over y, x, z_lo).
Axes of the slice: x: 4, y: 4, z: 8 (z_hi: 2, z_lo: 4; z = z_hi * 4 + z_lo), core: 2. Of those that a mesh axis runs over, the one named last changes fastest.
Arguments:
- activations: bfloat16 [4, 1024, 5120], P('island', 'tensor'), may hold values from -30 to 30, as said below
- cotangent: bfloat16 [4, 1024, 5120], P('island', 'tensor'), may hold values from -24 to 24
- gate_weight: bfloat16 [4, 6912, 5120], P('island', 'tensor'), may hold values from -6 to 6
- up_weight: bfloat16 [4, 6912, 5120], P('island', 'tensor'), may hold values from -6 to 6
- down_weight: bfloat16 [4, 6912, 5120], P('island', 'tensor'), may hold values from -6 to 6
- gate_control: bfloat16 [4, 6912, 5120], P('island', 'tensor'), may hold values from -4 to 4
- up_control: bfloat16 [4, 6912, 5120], P('island', 'tensor'), may hold values from -4 to 4
- down_control: bfloat16 [4, 6912, 5120], P('island', 'tensor'), may hold values from -4 to 4
Outputs:
- gate_new: bfloat16 [6912, 5120], P('tensor')
- up_new: bfloat16 [6912, 5120], P('tensor')
- down_new: bfloat16 [6912, 5120], P('tensor')
- gate_control_new: bfloat16 [4, 6912, 5120], P('island', 'tensor')
- up_control_new: bfloat16 [4, 6912, 5120], P('island', 'tensor')
- down_control_new: bfloat16 [4, 6912, 5120], P('island', 'tensor')
Inputs may be any that keep to these rules, and one draw needn't show every extreme that they name: `activations`: real values; columns and tokens carry different scales.
All inputs are finite; a program needn't handle non-finite values.
Results may differ from a plain program's by a relative error of at most 0.0095.
Values may be sent and summed in bfloat16 or wider, within the bound.
No kernel may reach another device: no remote copies, remote signals or barrier semaphores. Data moves between devices by JAX's collectives and lax.ppermute only.
A program may use at most 128 MiB of HBM per device.

v0:
```python
import jax
import jax.numpy as jnp
from jax import lax
from jax.sharding import PartitionSpec as P

D = 5120
FF = 6912
EPSILON = 1e-06
STEP_SIZE = 1.0
PROX_PROB = 0.5


def contract_first(left, right):
    return lax.dot_general(
        left, right, (((0,), (0,)), ((), ())), preferred_element_type=jnp.float32
    )


def contract_last(left, right):
    return lax.dot_general(
        left, right, (((1,), (1,)), ((), ())), preferred_element_type=jnp.float32
    )


def normalize(rows):
    wide = rows.astype(jnp.float32)
    mean_square = jnp.mean(wide * wide, axis=-1, keepdims=True)
    return (wide * lax.rsqrt(mean_square + EPSILON)).astype(jnp.bfloat16)


def block_grads(normed, cot_rows, gate_w, up_w, down_w):
    d_scale = D ** (-0.5)
    f_scale = FF ** (-0.5)
    gate_proj = contract_last(normed, gate_w) * d_scale
    up_proj = contract_last(normed, up_w) * d_scale
    sigmoid_gate = jax.nn.sigmoid(gate_proj)
    activated = gate_proj * sigmoid_gate
    hidden = (activated * up_proj).astype(jnp.bfloat16)
    grad_down = contract_first(hidden, cot_rows) * f_scale
    grad_hidden = contract_last(cot_rows, down_w) * f_scale
    grad_gatepre = (
        grad_hidden * up_proj * sigmoid_gate * (1.0 + gate_proj * (1.0 - sigmoid_gate))
    ).astype(jnp.bfloat16)
    grad_uppre = (grad_hidden * activated).astype(jnp.bfloat16)
    grad_gate = contract_first(grad_gatepre, normed) * d_scale
    grad_up = contract_first(grad_uppre, normed) * d_scale
    return (grad_gate, grad_up, grad_down)


def prox_parts(weight, control, grad):
    control_wide = control.astype(jnp.float32)
    local = weight.astype(jnp.float32) - STEP_SIZE * (grad - control_wide)
    return (local, (local - STEP_SIZE / PROX_PROB * control_wide).astype(jnp.bfloat16))


def fresh_control(control, mean_rounded, local):
    wide = control.astype(jnp.float32) + PROX_PROB / STEP_SIZE * (
        mean_rounded.astype(jnp.float32) - local
    )
    return wide.astype(jnp.bfloat16)[None]


def per_device(
    activations,
    cotangent,
    gate_weight,
    up_weight,
    down_weight,
    gate_control,
    up_control,
    down_control,
):
    own_rows = activations[0]
    own_cot = cotangent[0]
    normed = lax.all_gather(normalize(own_rows), "tensor", axis=0, tiled=True)
    whole_cot = lax.all_gather(own_cot, "tensor", axis=0, tiled=True)
    grad_gate, grad_up, grad_down = block_grads(
        normed, whole_cot, gate_weight[0], up_weight[0], down_weight[0]
    )
    local_gate, term_gate = prox_parts(gate_weight[0], gate_control[0], grad_gate)
    local_up, term_up = prox_parts(up_weight[0], up_control[0], grad_up)
    local_down, term_down = prox_parts(down_weight[0], down_control[0], grad_down)
    count = lax.axis_size("island")
    total_gate, total_up, total_down = (
        lax.psum(term_gate, "island").astype(jnp.float32),
        lax.psum(term_up, "island").astype(jnp.float32),
        lax.psum(term_down, "island").astype(jnp.float32),
    )
    mean_gate = (total_gate / count).astype(jnp.bfloat16)
    mean_up = (total_up / count).astype(jnp.bfloat16)
    mean_down = (total_down / count).astype(jnp.bfloat16)
    new_gate_control = fresh_control(gate_control[0], mean_gate, local_gate)
    new_up_control = fresh_control(up_control[0], mean_up, local_up)
    new_down_control = fresh_control(down_control[0], mean_down, local_down)
    return (mean_gate, mean_up, mean_down, new_gate_control, new_up_control, new_down_control)


def solution(mesh):
    placed = (
        P("island", "tensor", None),
        P("island", "tensor", None),
        P("island", "tensor", None),
        P("island", "tensor", None),
        P("island", "tensor", None),
        P("island", "tensor", None),
        P("island", "tensor", None),
        P("island", "tensor", None),
    )
    return jax.shard_map(
        per_device,
        mesh=mesh,
        in_specs=placed,
        out_specs=(
            P("tensor", None),
            P("tensor", None),
            P("tensor", None),
            P("island", "tensor", None),
            P("island", "tensor", None),
            P("island", "tensor", None),
        ),
        check_vma=False,
    )
```

profile of v0, /device:TPU:1, one launch (start us, length us, event | category | flops | bytes accessed | tf_op | source)
XLA Modules:
  0.0 956.3 jit_solution(8239383202195098988)
XLA Ops:
  7.2 0.0 all-gather.4.cloned.1.call-start
  7.2 1.1 fusion.36
  8.3 1.7 fusion.37
  10.0 0.0 all-gather.4.cloned.1.call-update
  10.0 0.0 all-gather.6.cloned.1.call-start
  10.0 0.7 all-gather.6.cloned.1.call-update
  10.8 0.0 copy-start.11
  10.8 0.0 all-reduce.3.cloned.1.call-start
  10.8 343.7 %all-gather.4.cloned.1.call-done = bf16[1024,5120]{1,0:T(8,128)(2,1)} async-done(((bf16[16,5120]{1,0:T(8,128)(2,1)}), bf16[1024,5120]{1,0:T(8,128)(2,1)}) %all-gather.4.cloned.1.call-update) | async-done | bytes 10485776 | tf_op jit(solution)/shard_map/all_gather | solution.py:75
  354.5 0.0 copy-start
  354.5 7.9 convolution_multiply_fusion.2
  362.4 0.0 copy-done.11
  362.4 0.0 copy-done
  362.4 0.0 copy-start.8
  362.4 3.5 convolution_multiply_fusion.3
  366.0 367.8 %all-gather.6.cloned.1.call-done = bf16[1,1024,5120]{2,1,0:T(8,128)(2,1)} async-done(((bf16[1,16,5120]{2,1,0:T(8,128)(2,1)}), bf16[1,1024,5120]{2,1,0:T(8,128)(2,1)}) %all-gather.6.cloned.1.call-update) | async-done | bytes 10485776 | tf_op jit(solution)/shard_map/all_gather | solution.py:76
  733.7 0.0 copy-done.8
  733.7 0.0 copy-start.6
  733.7 0.0 copy-start.9
  733.7 0.0 slice-start
  733.8 0.0 slice-start.1
  733.8 7.6 fusion.26
  741.4 0.0 copy-done.6
  741.4 0.0 copy-done.9
  741.4 0.0 slice-start.2
  741.4 0.0 copy-start.2
  741.4 0.0 copy-start.10
  741.4 7.5 fusion.24
  748.9 0.0 slice-done
  748.9 0.0 slice-done.1
  748.9 0.0 slice-done.2
  748.9 0.0 copy-done.2
  748.9 0.0 copy-done.10
  749.0 0.0 copy-start.4
  749.0 0.0 copy-start.12
  749.0 4.4 fusion.18
  753.4 0.0 copy-done.4
  753.4 0.0 copy-done.12
  753.4 4.5 fusion.21
  757.8 0.0 copy-start.3
  757.8 0.0 all-reduce.3.cloned.1.call-update
  757.9 184.1 %all-reduce.3.cloned.1.call-done = (bf16[108,5120]{1,0:T(8,128)(2,1)}, bf16[108,5120]{1,0:T(8,128)(2,1)}, bf16[108,5120]{1,0:T(8,128)(2,1)}) async-done(((bf16[108,5120]{1,0:T(8,128)(2,1)}, bf16[108,5120]{1,0:T(8,128)(2,1)}, bf16[108,5120]{1,0:T(8,128)(2,1)}), (bf16[108,5120]{1,0:T(8,128)(2,1)}, bf16[108,5120]{1,0:T(8,128)(2,1)}, bf16[108,5120]{1,0:T(8,128)(2,1)})) %all-reduce.3.cloned.1.call-update) | async-done | bytes 3317776 | tf_op jit(solution)/shard_map/psum | solution.py:85
  941.9 0.0 copy-done.3
  941.9 0.0 copy-start.1
  941.9 0.0 copy-start.5
  942.0 0.0 copy-start.7
  942.0 0.0 copy-start.13
  942.0 0.0 copy-start.14
  942.0 4.0 fusion.31
  946.0 0.0 copy-done.1
  946.0 0.0 copy-done.5
  946.0 0.0 copy-done.7
  946.0 0.0 copy-done.13
  946.0 0.7 copy-done.14
  946.8 3.0 fusion.29
  (2 shorter events, 0.0 us)
Async XLA Ops:
  7.2 347.3 %all-gather.4.cloned.1.call-start = ((), (), s32[]{:S(2)}) async-start(), calls=%async_computation | async-start | bytes 10649600 | tf_op jit(solution)/shard_map/all_gather | solution.py:75
  10.0 723.7 %all-gather.6.cloned.1.call-start = ((), (), s32[]{:S(2)}) async-start(), calls=%async_computation.1 | async-start | bytes 10649600 | tf_op jit(solution)/shard_map/all_gather | solution.py:76
  10.8 351.7 %copy-start.11 = (bf16[1,108,5120]{2,1,0:T(8,128)(2,1)S(1)}, bf16[1,108,5120]{2,1,0:T(8,128)(2,1)}, u32[]{:S(2)}) copy-start(bf16[1,108,5120]{2,1,0:T(8,128)(2,1)} %param.11) | copy-start | bytes 3317764
  10.8 931.2 %all-reduce.3.cloned.1.call-start = ((), (), s32[]{:S(2)}) async-start(), calls=%async_computation.2 | async-start | bytes 6881280 | tf_op jit(solution)/shard_map/psum | solution.py:85
  354.5 7.9 copy-start
  362.4 371.3 %copy-start.8 = (bf16[1,108,5120]{2,1,0:T(8,128)(2,1)S(1)}, bf16[1,108,5120]{2,1,0:T(8,128)(2,1)}, u32[]{:S(2)}) copy-start(bf16[1,108,5120]{2,1,0:T(8,128)(2,1)} %param.12) | copy-start | bytes 3317764
  733.7 7.6 copy-start.6
  733.7 7.7 copy-start.9
  733.7 15.2 %slice-start = ((s8[10485760]{0:T(1024)(128)(4,1)}), s8[4194304]{0:T(1024)(128)(4,1)S(1)}, s32[]{:S(2)}) async-start(s8[10485760]{0:T(1024)(128)(4,1)} %bitcast.56), calls=%async_computation.3 | async-start | bytes 8388608
  733.8 15.2 %slice-start.1 = ((s8[10485760]{0:T(1024)(128)(4,1)}), s8[4194304]{0:T(1024)(128)(4,1)S(1)}, s32[]{:S(2)}) async-start(s8[10485760]{0:T(1024)(128)(4,1)} %bitcast.56), calls=%async_computation.4 | async-start | bytes 8388608
  741.4 7.5 slice-start.2
  741.4 7.5 copy-start.2
  741.4 7.5 copy-start.10
  749.0 4.4 copy-start.4
  749.0 4.4 copy-start.12
  757.8 184.1 %copy-start.3 = (bf16[1,108,5120]{2,1,0:T(8,128)(2,1)S(1)}, bf16[1,108,5120]{2,1,0:T(8,128)(2,1)}, u32[]{:S(2)}) copy-start(bf16[1,108,5120]{2,1,0:T(8,128)(2,1)} %param.13) | copy-start | bytes 3317764
  941.9 4.1 copy-start.1
  941.9 4.1 copy-start.5
  942.0 4.1 copy-start.7
  942.0 4.1 copy-start.13
  942.0 4.8 copy-start.14
Sparse Core Ops, SparseCore 0:
  10.3 344.1 all-gather.3
  356.3 377.4 all-gather.5
  758.0 183.9 all-reduce.2
where the time goes:
time: 956 us
  waiting for transfers between devices  896 us (94%)
  matrix products  35.3 us (4%)
  between operations  13.9 us (1%)
  other arithmetic  9.76 us (1%)
    all_gather x1, waiting for transfers between devices, per_device(): whole_cot = lax.all_gather(own_cot, 'tensor', axis=0, tiled=True)  368 us
    all_gather x1, waiting for transfers between devices, per_device(): normed = lax.all_gather(normalize(own_rows), 'tensor', axis=0, tiled=True)  344 us
    psum x1, waiting for transfers between devices, per_device(): lax.psum(term_gate, 'island').astype(jnp.float32)  184 us
  transfers between devices with their start and end apart: 3, of which 3 were waited for; matrix products, arithmetic and copies ran while one was open for 1% of the time, Pallas kernels for 0%

commit v1 on v0

--- a/solution.py
+++ b/solution.py
@@ -72,7 +72,10 @@
 ):
     own_rows = activations[0]
     own_cot = cotangent[0]
-    normed = lax.all_gather(normalize(own_rows), "tensor", axis=0, tiled=True)
+    normed = jnp.concatenate(
+        lax.all_to_all(jnp.stack([normalize(own_rows)] * lax.axis_size("tensor")), "tensor", 0, 0),
+        axis=0,
+    )
     whole_cot = lax.all_gather(own_cot, "tensor", axis=0, tiled=True)
     grad_gate, grad_up, grad_down = block_grads(
         normed, whole_cot, gate_weight[0], up_weight[0], down_weight[0]

time: 956 us -> 701 us (0.73)
  waiting for transfers between devices: 896 us -> 615 us
  starting transfers between devices: 0.12 us -> 13 us
    all_to_all x0 -> x1, waiting for transfers between devices: none -> 410 us  [per_device(): lax.all_to_all(jnp.stack([normalize(own_rows)] * lax.axis_size('tensor'))...]
    all_gather x1 -> x0, waiting for transfers between devices: 344 us -> none  [per_device(): normed = lax.all_gather(normalize(own_rows), 'tensor', axis=0, tiled=True)]
    all_gather x1, waiting for transfers between devices: 368 us -> 35.9 us  [per_device(): whole_cot = lax.all_gather(own_cot, 'tensor', axis=0, tiled=True)]
    psum x1, waiting for transfers between devices: 184 us -> 169 us  [per_device(): lax.psum(term_gate, 'island').astype(jnp.float32)]
    all_to_all x0 -> x1, starting transfers between devices: none -> 12.9 us  [per_device(): lax.all_to_all(jnp.stack([normalize(own_rows)] * lax.axis_size('tensor'))...]
  transfers between devices with their start and end apart: 3 -> 3, of which waited for: 3 -> 3; matrix products, arithmetic and copies ran while one was open for 1% -> 2% of each run, Pallas kernels for 0% -> 0%
where the time goes in v1:
time: 701 us
  waiting for transfers between devices  615 us (88%)
  matrix products  43.1 us (6%)
  between operations  14.2 us (2%)
  starting transfers between devices  13 us (2%)
  other arithmetic  9.1 us (1%)
    all_to_all x1, waiting for transfers between devices, per_device(): lax.all_to_all(jnp.stack([normalize(own_rows)] * lax.axis_size('tensor'))...  410 us
    psum x1, waiting for transfers between devices, per_device(): lax.psum(term_gate, 'island').astype(jnp.float32)  169 us
    all_gather x1, waiting for transfers between devices, per_device(): whole_cot = lax.all_gather(own_cot, 'tensor', axis=0, tiled=True)  35.9 us
    dot_general x3, matrix products, contract_last(): lax.dot_general(left, right, (((1,), (1,)), ((), ())), preferred_element_...  22.8 us
    dot_general x3, matrix products, contract_first(): lax.dot_general(left, right, (((0,), (0,)), ((), ())), preferred_element_...  20.3 us
  transfers between devices with their start and end apart: 3, of which 3 were waited for; matrix products, arithmetic and copies ran while one was open for 2% of the time, Pallas kernels for 0%

profile of v1, /device:TPU:1, one launch (start us, length us, event | category | flops | bytes accessed | tf_op | source)
XLA Modules:
  0.0 700.7 jit_solution(12630212150312607855)
XLA Ops:
  7.2 1.1 fusion.36
  8.2 1.0 fusion.39
  9.3 5.2 stack.5
  14.5 0.0 copy-start.9
  14.5 12.9 %all-to-all-start = ((bf16[64,16,5120]{2,1,0:T(8,128)(2,1)}), bf16[64,16,5120]{2,1,0:T(8,128)(2,1)}, u32[]{:S(2)}, u32[]{:S(2)}) async-start(bf16[64,16,5120]{2,1,0:T(8,128)(2,1)} %stack.5), calls=%async_computation | async-start | bytes 20971520 | tf_op jit(solution)/shard_map/all_to_all | solution.py:76
  27.4 0.0 all-gather.3.cloned.1.call-start
  27.5 0.7 all-gather.3.cloned.1.call-update
  28.2 0.0 all-reduce.3.cloned.1.call-start
  28.2 410.1 %all-to-all-done = bf16[64,16,5120]{2,1,0:T(8,128)(2,1)} async-done(((bf16[64,16,5120]{2,1,0:T(8,128)(2,1)}), bf16[64,16,5120]{2,1,0:T(8,128)(2,1)}, u32[]{:S(2)}, u32[]{:S(2)}) %all-to-all-start) | async-done | bytes 10485792 | tf_op jit(solution)/shard_map/all_to_all | solution.py:76
  438.3 0.0 copy-done.9
  438.3 0.0 copy-start.7
  438.3 7.6 %convolution_multiply_fusion.2 = f32[1024,108]{0,1:T(8,128)S(1)} fusion(bf16[1024,5120]{1,0:T(8,128)(2,1)} %bitcast.4, bf16[1,108,5120]{2,1,0:T(8,128)(2,1)S(1)} %copy-done.9), kind=kOutput, calls=%fused_computation.31 | convolution fusion | flops 1132572672 | bytes 12034048 | tf_op jit(solution)/shard_map/dot_general | solution.py:20
  445.9 0.0 copy-done.7
  445.9 0.0 copy-start.11
  445.9 7.6 %convolution_multiply_fusion.3 = f32[1024,108]{0,1:T(8,128)S(1)} fusion(bf16[1024,5120]{1,0:T(8,128)(2,1)} %bitcast.4, bf16[1,108,5120]{2,1,0:T(8,128)(2,1)S(1)} %copy-done.7), kind=kOutput, calls=%fused_computation.32 | convolution fusion | flops 1132572672 | bytes 12034048 | tf_op jit(solution)/shard_map/dot_general | solution.py:20
  453.5 35.9 %all-gather.3.cloned.1.call-done = bf16[1,1024,5120]{2,1,0:T(8,128)(2,1)} async-done(((bf16[1,16,5120]{2,1,0:T(8,128)(2,1)}), bf16[1,1024,5120]{2,1,0:T(8,128)(2,1)}) %all-gather.3.cloned.1.call-update) | async-done | bytes 10485776 | tf_op jit(solution)/shard_map/all_gather | solution.py:79
  489.4 0.0 copy-done.11
  489.4 0.0 copy-start.3
  489.4 0.0 copy-start.8
  489.4 7.6 %fusion.26 = f32[1024,108]{0,1:T(8,128)S(1)} fusion(bf16[1,1024,5120]{2,1,0:T(8,128)(2,1)} %all-gather.3.cloned.1.call-done, bf16[1,108,5120]{2,1,0:T(8,128)(2,1)S(1)} %copy-done.11), kind=kOutput, calls=%fused_computation.33 | convolution fusion | flops 1132572672 | bytes 12034048 | tf_op jit(solution)/shard_map/dot_general | solution.py:20
  497.0 0.0 copy-done.3
  497.0 0.0 copy-done.8
  497.1 0.0 copy-start.1
  497.1 0.0 copy-start.10
  497.1 0.0 slice-start
  497.1 0.0 slice-start.1
  497.1 7.5 %fusion.21 = (bf16[108,5120]{1,0:T(8,128)(2,1)}, f32[108,5120]{1,0:T(8,128)S(1)}) fusion(bf16[1,108,5120]{2,1,0:T(8,128)(2,1)S(1)} %copy-done.3, bf16[1024,5120]{1,0:T(8,128)(2,1)} %bitcast.4, f32[1024,108]{0,1:T(8,128)S(1)} %fusion.26, f32[1024,108]{0,1:T(8,128)S(1)} %convolution_multiply_fusion.2, bf16[1,108,5120]{2,1,0:T(8,128)(2,1)S(1)} %copy-done.8), kind=kOutput, calls=%fused_computation.23 | convolution fusion | flops 1137549312 | bytes 16900096 | tf_op jit(solution)/shard_map/dot_general | solution.py:14
  504.6 0.0 copy-done.1
  504.6 0.0 copy-done.10
  504.6 0.0 slice-start.2
  504.6 0.0 copy-start.5
  504.6 0.0 copy-start.12
  504.6 8.3 %fusion.18 = (bf16[108,5120]{1,0:T(8,128)(2,1)}, f32[108,5120]{1,0:T(8,128)}) fusion(bf16[1,108,5120]{2,1,0:T(8,128)(2,1)S(1)} %copy-done.1, bf16[1024,5120]{1,0:T(8,128)(2,1)} %bitcast.4, f32[1024,108]{0,1:T(8,128)S(1)} %convolution_multiply_fusion.2, f32[1024,108]{0,1:T(8,128)S(1)} %fusion.26, f32[1024,108]{0,1:T(8,128)S(1)} %convolution_multiply_fusion.3, ...), kind=kOutput, calls=%fused_computation.20 | convolution fusion | flops 1137991680 | bytes 17342464 | tf_op jit(solution)/shard_map/dot_general | solution.py:14
  512.9 0.0 slice-done
  513.0 0.0 slice-done.1
  513.0 0.0 slice-done.2
  513.0 0.0 copy-done.5
  513.0 0.0 copy-done.12
  513.0 4.5 fusion.24
  517.4 0.0 copy-start.2
  517.4 0.0 all-reduce.3.cloned.1.call-update
  517.5 168.6 %all-reduce.3.cloned.1.call-done = (bf16[108,5120]{1,0:T(8,128)(2,1)}, bf16[108,5120]{1,0:T(8,128)(2,1)}, bf16[108,5120]{1,0:T(8,128)(2,1)}) async-done(((bf16[108,5120]{1,0:T(8,128)(2,1)}, bf16[108,5120]{1,0:T(8,128)(2,1)}, bf16[108,5120]{1,0:T(8,128)(2,1)}), (bf16[108,5120]{1,0:T(8,128)(2,1)}, bf16[108,5120]{1,0:T(8,128)(2,1)}, bf16[108,5120]{1,0:T(8,128)(2,1)})) %all-reduce.3.cloned.1.call-update) | async-done | bytes 3317776 | tf_op jit(solution)/shard_map/psum | solution.py:88
  686.0 0.0 copy-done.2
  686.1 0.0 copy-start
  686.1 0.0 copy-start.4
  686.1 0.0 copy-start.6
  686.1 0.0 copy-start.13
  686.1 0.0 copy-start.14
  686.1 4.0 fusion.31
  690.1 0.0 copy-done
  690.1 0.0 copy-done.4
  690.1 0.0 copy-done.6
  690.1 0.0 copy-done.13
  690.1 0.7 copy-done.14
  690.9 3.0 fusion.29
  (2 shorter events, 0.0 us)
Async XLA Ops:
  14.5 423.8 %copy-start.9 = (bf16[1,108,5120]{2,1,0:T(8,128)(2,1)S(1)}, bf16[1,108,5120]{2,1,0:T(8,128)(2,1)}, u32[]{:S(2)}) copy-start(bf16[1,108,5120]{2,1,0:T(8,128)(2,1)} %param.10) | copy-start | bytes 3317764
  14.5 423.8 %all-to-all-start = ((bf16[64,16,5120]{2,1,0:T(8,128)(2,1)}), bf16[64,16,5120]{2,1,0:T(8,128)(2,1)}, u32[]{:S(2)}, u32[]{:S(2)}) async-start(bf16[64,16,5120]{2,1,0:T(8,128)(2,1)} %stack.5), calls=%async_computation | async-start | bytes 20971520 | tf_op jit(solution)/shard_map/all_to_all | solution.py:76
  27.4 462.0 %all-gather.3.cloned.1.call-start = ((), (), s32[]{:S(2)}) async-start(), calls=%async_computation.1 | async-start | bytes 10649600 | tf_op jit(solution)/shard_map/all_gather | solution.py:79
  28.2 657.9 %all-reduce.3.cloned.1.call-start = ((), (), s32[]{:S(2)}) async-start(), calls=%async_computation.2 | async-start | bytes 6881280 | tf_op jit(solution)/shard_map/psum | solution.py:88
  438.3 7.6 %copy-start.7 = (bf16[1,108,5120]{2,1,0:T(8,128)(2,1)S(1)}, bf16[1,108,5120]{2,1,0:T(8,128)(2,1)}, u32[]{:S(2)}) copy-start(bf16[1,108,5120]{2,1,0:T(8,128)(2,1)} %param.11) | copy-start | bytes 3317764
  445.9 43.5 %copy-start.11 = (bf16[1,108,5120]{2,1,0:T(8,128)(2,1)S(1)}, bf16[1,108,5120]{2,1,0:T(8,128)(2,1)}, u32[]{:S(2)}) copy-start(bf16[1,108,5120]{2,1,0:T(8,128)(2,1)} %param.12) | copy-start | bytes 3317764
  489.4 7.6 %copy-start.3 = (bf16[1,108,5120]{2,1,0:T(8,128)(2,1)S(1)}, bf16[1,108,5120]{2,1,0:T(8,128)(2,1)}, u32[]{:S(2)}) copy-start(bf16[1,108,5120]{2,1,0:T(8,128)(2,1)} %param.14) | copy-start | bytes 3317764
  489.4 7.6 %copy-start.8 = (bf16[1,108,5120]{2,1,0:T(8,128)(2,1)S(1)}, bf16[1,108,5120]{2,1,0:T(8,128)(2,1)}, u32[]{:S(2)}) copy-start(bf16[1,108,5120]{2,1,0:T(8,128)(2,1)} %param.11) | copy-start | bytes 3317764
  497.1 7.6 %copy-start.1 = (bf16[1,108,5120]{2,1,0:T(8,128)(2,1)S(1)}, bf16[1,108,5120]{2,1,0:T(8,128)(2,1)}, u32[]{:S(2)}) copy-start(bf16[1,108,5120]{2,1,0:T(8,128)(2,1)} %param.13) | copy-start | bytes 3317764
  497.1 7.5 %copy-start.10 = (bf16[1,108,5120]{2,1,0:T(8,128)(2,1)S(1)}, bf16[1,108,5120]{2,1,0:T(8,128)(2,1)}, u32[]{:S(2)}) copy-start(bf16[1,108,5120]{2,1,0:T(8,128)(2,1)} %param.10) | copy-start | bytes 3317764
  497.1 15.9 %slice-start = ((s8[10485760]{0:T(1024)(128)(4,1)}), s8[4194304]{0:T(1024)(128)(4,1)S(1)}, s32[]{:S(2)}) async-start(s8[10485760]{0:T(1024)(128)(4,1)} %bitcast.55), calls=%async_computation.3 | async-start | bytes 8388608
  497.1 15.9 %slice-start.1 = ((s8[10485760]{0:T(1024)(128)(4,1)}), s8[4194304]{0:T(1024)(128)(4,1)S(1)}, s32[]{:S(2)}) async-start(s8[10485760]{0:T(1024)(128)(4,1)} %bitcast.55), calls=%async_computation.4 | async-start | bytes 8388608
  504.6 8.3 %slice-start.2 = ((s8[10485760]{0:T(1024)(128)(4,1)}), s8[2097152]{0:T(1024)(128)(4,1)S(1)}, s32[]{:S(2)}) async-start(s8[10485760]{0:T(1024)(128)(4,1)} %bitcast.55), calls=%async_computation.5 | async-start | bytes 4194304
  504.6 8.3 %copy-start.5 = (bf16[1,108,5120]{2,1,0:T(8,128)(2,1)S(1)}, bf16[1,108,5120]{2,1,0:T(8,128)(2,1)}, u32[]{:S(2)}) copy-start(bf16[1,108,5120]{2,1,0:T(8,128)(2,1)} %param.15) | copy-start | bytes 3317764
  504.6 8.3 %copy-start.12 = (bf16[1,108,5120]{2,1,0:T(8,128)(2,1)S(1)}, bf16[1,108,5120]{2,1,0:T(8,128)(2,1)}, u32[]{:S(2)}) copy-start(bf16[1,108,5120]{2,1,0:T(8,128)(2,1)} %param.12) | copy-start | bytes 3317764
  517.4 168.6 %copy-start.2 = (bf16[1,108,5120]{2,1,0:T(8,128)(2,1)S(1)}, bf16[1,108,5120]{2,1,0:T(8,128)(2,1)}, u32[]{:S(2)}) copy-start(bf16[1,108,5120]{2,1,0:T(8,128)(2,1)} %param.13) | copy-start | bytes 3317764
  686.1 4.1 copy-start
  686.1 4.1 copy-start.4
  686.1 4.1 copy-start.6
  686.1 4.1 copy-start.13
  686.1 4.8 copy-start.14
Sparse Core Ops, SparseCore 0:
  30.0 459.3 all-gather.2
  517.6 168.4 all-reduce.2
